TPU v7x, 32 devices: a whole 2x2x4 slice. The times are simulated.
32 devices in a mesh: sx: 16 (over z, y, x), sy: 2 (over core).
Axes of the slice: x: 2, y: 2, z: 4, core: 2. Of those that a mesh axis runs over, the one named last changes fastest.
Arguments:
- snapshots: bfloat16 [1024, 3, 32, 256], P(None, None, 'sx', 'sy'), may hold values from -6 to 6
- quad_weight: float32 [3, 32, 256], P(None, 'sx', 'sy'), may hold values from 0.5 to 1200
- mode_guess: float32 [16, 64, 2, 8], replicated, may hold values from -6 to 6
- bins: int32 [16], replicated, may hold values from 1 to 127
- starts: int32 [64], replicated, may hold values from 0 to 768
Outputs:
- modes: float32 [16, 2, 8, 3, 32, 256], P(None, None, None, None, 'sx', 'sy')
- energy: float32 [16, 8], replicated
All inputs are finite; a program needn't handle non-finite values.
Results may differ from a plain program's by a relative error of at most 0.0024.
Values may be sent and summed in bfloat16 or wider, within the bound.
A program may use at most 64 MiB of HBM per device.

v0:
```python
import jax
import jax.numpy as jnp
from jax import lax
from jax.sharding import PartitionSpec as P

NFFT = 256


EPS = 1e-06


def make_twiddle(bins):
    steps = jnp.arange(NFFT, dtype=jnp.int32)
    window = 0.5 - 0.5 * jnp.cos(2.0 * jnp.pi * steps.astype(jnp.float32) / NFFT)
    norm_c = 1.0 / jnp.sqrt(jnp.sum(window * window))
    phase = bins[:, None] * steps[None, :] % NFFT
    angle = 2.0 * jnp.pi * phase.astype(jnp.float32) / NFFT
    twid = jnp.stack(
        [norm_c * window * jnp.cos(angle), -(norm_c * window) * jnp.sin(angle)], axis=1
    )
    return twid.astype(jnp.bfloat16)


def row_terms(rows, start, guess, nblock):
    count = rows.shape[0]
    nbins = guess.shape[0]
    hp = lax.Precision.HIGHEST
    which = (start + jnp.arange(count, dtype=jnp.int32)) // nblock
    onehot = (which[:, None] == jnp.arange(nbins, dtype=jnp.int32)[None, :]).astype(jnp.float32)
    picked = jnp.einsum("rf,fcpn->rcpn", onehot, guess, precision=hp)
    gram_re = rows[:, :nblock]
    gram_im = rows[:, nblock:]
    zre = jnp.einsum("rc,rcn->rn", gram_re, picked[:, :, 0], precision=hp) - jnp.einsum(
        "rc,rcn->rn", gram_im, picked[:, :, 1], precision=hp
    )
    zim = jnp.einsum("rc,rcn->rn", gram_re, picked[:, :, 1], precision=hp) + jnp.einsum(
        "rc,rcn->rn", gram_im, picked[:, :, 0], precision=hp
    )
    partial_norm = jnp.einsum("rf,rn->fn", onehot, zre * zre + zim * zim, precision=hp)
    return (zre, zim, partial_norm, onehot)


def finish_rows(zre, zim, norms, onehot):
    row_norm = jnp.dot(onehot, norms, precision=lax.Precision.HIGHEST)
    inv = lax.rsqrt(row_norm + EPS)
    return jnp.concatenate([zre * inv, zim * inv], axis=-1).astype(jnp.bfloat16)


def shards(snapshots, quad_weight, mode_guess, bins, starts):
    length, nvar, cols_x, cols_y = snapshots.shape
    nbins = bins.shape[0]
    nblock = starts.shape[0]
    nmode = mode_guess.shape[-1]
    points = nvar * cols_x * cols_y
    local_sq = jnp.sum(
        jnp.square(snapshots.astype(jnp.float32)) * quad_weight[None], axis=(0, 2, 3)
    )
    total_sq = lax.psum(local_sq, ("sx", "sy"))
    grid_points = cols_x * cols_y * lax.axis_size("sx") * lax.axis_size("sy")
    scale = lax.rsqrt(total_sq / (length * grid_points) + EPS)
    colscale = (scale[:, None, None] * jnp.sqrt(quad_weight)).reshape(points)
    twid = make_twiddle(bins).reshape(nbins * 2, NFFT)
    flat = snapshots.reshape(length, points)
    group = 8

    def block_step(number):
        first_block = lax.dynamic_slice_in_dim(starts, number * group, group)
        times = first_block[:, None] + jnp.arange(NFFT, dtype=jnp.int32)[None, :]
        windows = jnp.take(flat, times, axis=0)
        qhat = jnp.einsum("qt,btx->bqx", twid, windows, preferred_element_type=jnp.float32)
        return (qhat * colscale[None, None, :]).astype(jnp.bfloat16)

    blocks = lax.map(block_step, jnp.arange(nblock // group, dtype=jnp.int32))
    blocks = blocks.reshape(nblock, nbins, 2, points)
    ydata = jnp.transpose(blocks, (1, 2, 0, 3)).reshape(nbins, 2 * nblock, points)
    gram = jnp.einsum("fax,fbx->fab", ydata, ydata, preferred_element_type=jnp.float32)
    gram_re = gram[:, :nblock, :nblock] + gram[:, nblock:, nblock:]
    gram_im = gram[:, :nblock, nblock:] - gram[:, nblock:, :nblock]
    local_gram = jnp.concatenate([gram_re, gram_im], axis=-1).reshape(nbins * nblock, 2 * nblock)
    denom = 3.0 * grid_points
    halves = lax.psum_scatter(
        local_gram.astype(jnp.bfloat16), "sy", scatter_dimension=0, tiled=True
    ).astype(jnp.float32)
    owned = lax.psum(halves, "sx") / denom
    first = lax.axis_index("sy") * owned.shape[0]
    zre, zim, partial_norm, onehot = row_terms(owned, first, mode_guess, nblock)
    norms = lax.psum(partial_norm, "sy")
    coef = lax.all_gather(finish_rows(zre, zim, norms, onehot), "sy", axis=0, tiled=True)
    energy = jnp.sqrt(norms / nblock)
    coef = coef.reshape(nbins, nblock, 2 * nmode)
    coef_re = coef[:, :, :nmode]
    coef_im = coef[:, :, nmode:]
    upper = jnp.concatenate([coef_re, coef_im], axis=-1)
    lower = jnp.concatenate([-coef_im, coef_re], axis=-1)
    stacked = jnp.concatenate([upper, lower], axis=1)
    modes = jnp.einsum("fan,fax->fnx", stacked, ydata, preferred_element_type=jnp.float32)
    return (modes.reshape(nbins, 2, nmode, nvar, cols_x, cols_y), energy)


def solution(mesh):
    return jax.shard_map(
        shards,
        mesh=mesh,
        in_specs=(P(None, None, "sx", "sy"), P(None, "sx", "sy"), P(), P(), P()),
        out_specs=(P(None, None, None, None, "sx", "sy"), P()),
        check_vma=False,
    )
```

profile of v0, /device:TPU:0, one launch (start us, length us, event | category | flops | bytes accessed | tf_op | source)
XLA Modules:
  0.0 293.6 jit_solution(9063561750180398225)
XLA Ops:
  9.5 3.9 %reshape.249 = bf16[1024,768]{1,0:T(8,128)(2,1)S(1)} reshape(bf16[1024,3,2,128]{3,2,1,0:T(2,128)(2,1)} %param.7) | data formatting | bytes 3145728 | tf_op jit(solution)/shard_map/reshape | solution.py:63
  13.4 2.4 multiply_reduce_fusion
  15.9 42.2 %psum.21 = f32[3]{0:T(128)S(1)} all-reduce(f32[3]{0:T(128)S(1)} %multiply_reduce_fusion), channel_id=1, replica_groups=mesh['sx'=16,'sy'=2] {'sx','sy'}, use_global_device_ids=true, to_apply=%region_2.0 | all-reduce | flops 3 | bytes 24 | tf_op jit(solution)/shard_map/psum | solution.py:58
  58.1 115.3 %while.10 = (s32[]{:T(128)}, bf16[8,8,32,768]{3,2,1,0:T(8,128)(2,1)}, s32[8]{0:T(128)S(1)}, s32[64]{0:T(128)S(1)}, bf16[1024,768]{1,0:T(8,128)(2,1)S(1)}, /*inde...) while((s32[]{:T(128)}, ...), condition=%wide.region_4.5_spmd, body=%wide.region_3.4_spmd.sunk | while | flops 102653960 | bytes 9910059 | solution.py:73
  59.6 9.4 %gather_fusion = bf16[2048,768]{1,0:T(8,128)(2,1)} fusion(bf16[1024,768]{1,0:T(8,128)(2,1)S(1)} %get-tuple-element.149, s32[2048]{0:T(1024)S(1)} %broadcast_clamp_fusion.2), kind=kCustom, calls=%fused_computation.clone.1 | custom fusion | bytes 6299648 | tf_op jit(solution)/shard_map/while/body/eval_jaxpr/jit(_take)/gather | solution.py:69
  69.0 3.5 %fusion.69 = bf16[8,8,32,768]{3,2,1,0:T(8,128)(2,1)} fusion(bf16[8,8,32,768]{3,2,1,0:T(8,128)(2,1)} %get-tuple-element.135, s32[]{:T(128)} %get-tuple-element.134, bf16[8,256,768]{2,1,0:T(8,128)(2,1)} %bitcast.58, pred[8,256]{1,0:T(8,128)(4,1)S(1)} %fusion.68, f32[768]{0:T(1024)S(1)} %mul.244, bf16[32,256]{1,0:T(8,128)(2,1)S(1)} %get-tuple-element.150), kind=kOutput, calls=%fused_computation.8.clone.1 | convolution fusion | flops 102629376 | bytes 3560960 | tf_op jit(solution)/shard_map/while/body/eval_jaxpr/qt,btx->bqx/dot_general | solution.py:70
  74.0 9.4 %gather_fusion = bf16[2048,768]{1,0:T(8,128)(2,1)} fusion(bf16[1024,768]{1,0:T(8,128)(2,1)S(1)} %get-tuple-element.149, s32[2048]{0:T(1024)S(1)} %broadcast_clamp_fusion.2), kind=kCustom, calls=%fused_computation.clone.1 | custom fusion | bytes 6299648 | tf_op jit(solution)/shard_map/while/body/eval_jaxpr/jit(_take)/gather | solution.py:69
  83.4 3.5 %fusion.69 = bf16[8,8,32,768]{3,2,1,0:T(8,128)(2,1)} fusion(bf16[8,8,32,768]{3,2,1,0:T(8,128)(2,1)} %get-tuple-element.135, s32[]{:T(128)} %get-tuple-element.134, bf16[8,256,768]{2,1,0:T(8,128)(2,1)} %bitcast.58, pred[8,256]{1,0:T(8,128)(4,1)S(1)} %fusion.68, f32[768]{0:T(1024)S(1)} %mul.244, bf16[32,256]{1,0:T(8,128)(2,1)S(1)} %get-tuple-element.150), kind=kOutput, calls=%fused_computation.8.clone.1 | convolution fusion | flops 102629376 | bytes 3560960 | tf_op jit(solution)/shard_map/while/body/eval_jaxpr/qt,btx->bqx/dot_general | solution.py:70
  88.4 9.4 %gather_fusion = bf16[2048,768]{1,0:T(8,128)(2,1)} fusion(bf16[1024,768]{1,0:T(8,128)(2,1)S(1)} %get-tuple-element.149, s32[2048]{0:T(1024)S(1)} %broadcast_clamp_fusion.2), kind=kCustom, calls=%fused_computation.clone.1 | custom fusion | bytes 6299648 | tf_op jit(solution)/shard_map/while/body/eval_jaxpr/jit(_take)/gather | solution.py:69
  97.8 3.5 %fusion.69 = bf16[8,8,32,768]{3,2,1,0:T(8,128)(2,1)} fusion(bf16[8,8,32,768]{3,2,1,0:T(8,128)(2,1)} %get-tuple-element.135, s32[]{:T(128)} %get-tuple-element.134, bf16[8,256,768]{2,1,0:T(8,128)(2,1)} %bitcast.58, pred[8,256]{1,0:T(8,128)(4,1)S(1)} %fusion.68, f32[768]{0:T(1024)S(1)} %mul.244, bf16[32,256]{1,0:T(8,128)(2,1)S(1)} %get-tuple-element.150), kind=kOutput, calls=%fused_computation.8.clone.1 | convolution fusion | flops 102629376 | bytes 3560960 | tf_op jit(solution)/shard_map/while/body/eval_jaxpr/qt,btx->bqx/dot_general | solution.py:70
  102.7 9.4 %gather_fusion = bf16[2048,768]{1,0:T(8,128)(2,1)} fusion(bf16[1024,768]{1,0:T(8,128)(2,1)S(1)} %get-tuple-element.149, s32[2048]{0:T(1024)S(1)} %broadcast_clamp_fusion.2), kind=kCustom, calls=%fused_computation.clone.1 | custom fusion | bytes 6299648 | tf_op jit(solution)/shard_map/while/body/eval_jaxpr/jit(_take)/gather | solution.py:69
  112.2 3.5 %fusion.69 = bf16[8,8,32,768]{3,2,1,0:T(8,128)(2,1)} fusion(bf16[8,8,32,768]{3,2,1,0:T(8,128)(2,1)} %get-tuple-element.135, s32[]{:T(128)} %get-tuple-element.134, bf16[8,256,768]{2,1,0:T(8,128)(2,1)} %bitcast.58, pred[8,256]{1,0:T(8,128)(4,1)S(1)} %fusion.68, f32[768]{0:T(1024)S(1)} %mul.244, bf16[32,256]{1,0:T(8,128)(2,1)S(1)} %get-tuple-element.150), kind=kOutput, calls=%fused_computation.8.clone.1 | convolution fusion | flops 102629376 | bytes 3560960 | tf_op jit(solution)/shard_map/while/body/eval_jaxpr/qt,btx->bqx/dot_general | solution.py:70
  117.1 9.4 %gather_fusion = bf16[2048,768]{1,0:T(8,128)(2,1)} fusion(bf16[1024,768]{1,0:T(8,128)(2,1)S(1)} %get-tuple-element.149, s32[2048]{0:T(1024)S(1)} %broadcast_clamp_fusion.2), kind=kCustom, calls=%fused_computation.clone.1 | custom fusion | bytes 6299648 | tf_op jit(solution)/shard_map/while/body/eval_jaxpr/jit(_take)/gather | solution.py:69
  126.6 3.5 %fusion.69 = bf16[8,8,32,768]{3,2,1,0:T(8,128)(2,1)} fusion(bf16[8,8,32,768]{3,2,1,0:T(8,128)(2,1)} %get-tuple-element.135, s32[]{:T(128)} %get-tuple-element.134, bf16[8,256,768]{2,1,0:T(8,128)(2,1)} %bitcast.58, pred[8,256]{1,0:T(8,128)(4,1)S(1)} %fusion.68, f32[768]{0:T(1024)S(1)} %mul.244, bf16[32,256]{1,0:T(8,128)(2,1)S(1)} %get-tuple-element.150), kind=kOutput, calls=%fused_computation.8.clone.1 | convolution fusion | flops 102629376 | bytes 3560960 | tf_op jit(solution)/shard_map/while/body/eval_jaxpr/qt,btx->bqx/dot_general | solution.py:70
  131.6 9.4 %gather_fusion = bf16[2048,768]{1,0:T(8,128)(2,1)} fusion(bf16[1024,768]{1,0:T(8,128)(2,1)S(1)} %get-tuple-element.149, s32[2048]{0:T(1024)S(1)} %broadcast_clamp_fusion.2), kind=kCustom, calls=%fused_computation.clone.1 | custom fusion | bytes 6299648 | tf_op jit(solution)/shard_map/while/body/eval_jaxpr/jit(_take)/gather | solution.py:69
  141.0 3.5 %fusion.69 = bf16[8,8,32,768]{3,2,1,0:T(8,128)(2,1)} fusion(bf16[8,8,32,768]{3,2,1,0:T(8,128)(2,1)} %get-tuple-element.135, s32[]{:T(128)} %get-tuple-element.134, bf16[8,256,768]{2,1,0:T(8,128)(2,1)} %bitcast.58, pred[8,256]{1,0:T(8,128)(4,1)S(1)} %fusion.68, f32[768]{0:T(1024)S(1)} %mul.244, bf16[32,256]{1,0:T(8,128)(2,1)S(1)} %get-tuple-element.150), kind=kOutput, calls=%fused_computation.8.clone.1 | convolution fusion | flops 102629376 | bytes 3560960 | tf_op jit(solution)/shard_map/while/body/eval_jaxpr/qt,btx->bqx/dot_general | solution.py:70
  146.0 9.4 %gather_fusion = bf16[2048,768]{1,0:T(8,128)(2,1)} fusion(bf16[1024,768]{1,0:T(8,128)(2,1)S(1)} %get-tuple-element.149, s32[2048]{0:T(1024)S(1)} %broadcast_clamp_fusion.2), kind=kCustom, calls=%fused_computation.clone.1 | custom fusion | bytes 6299648 | tf_op jit(solution)/shard_map/while/body/eval_jaxpr/jit(_take)/gather | solution.py:69
  155.4 3.6 %fusion.69 = bf16[8,8,32,768]{3,2,1,0:T(8,128)(2,1)} fusion(bf16[8,8,32,768]{3,2,1,0:T(8,128)(2,1)} %get-tuple-element.135, s32[]{:T(128)} %get-tuple-element.134, bf16[8,256,768]{2,1,0:T(8,128)(2,1)} %bitcast.58, pred[8,256]{1,0:T(8,128)(4,1)S(1)} %fusion.68, f32[768]{0:T(1024)S(1)} %mul.244, bf16[32,256]{1,0:T(8,128)(2,1)S(1)} %get-tuple-element.150), kind=kOutput, calls=%fused_computation.8.clone.1 | convolution fusion | flops 102629376 | bytes 3560960 | tf_op jit(solution)/shard_map/while/body/eval_jaxpr/qt,btx->bqx/dot_general | solution.py:70
  160.4 9.4 %gather_fusion = bf16[2048,768]{1,0:T(8,128)(2,1)} fusion(bf16[1024,768]{1,0:T(8,128)(2,1)S(1)} %get-tuple-element.149, s32[2048]{0:T(1024)S(1)} %broadcast_clamp_fusion.2), kind=kCustom, calls=%fused_computation.clone.1 | custom fusion | bytes 6299648 | tf_op jit(solution)/shard_map/while/body/eval_jaxpr/jit(_take)/gather | solution.py:69
  169.9 3.5 %fusion.69 = bf16[8,8,32,768]{3,2,1,0:T(8,128)(2,1)} fusion(bf16[8,8,32,768]{3,2,1,0:T(8,128)(2,1)} %get-tuple-element.135, s32[]{:T(128)} %get-tuple-element.134, bf16[8,256,768]{2,1,0:T(8,128)(2,1)} %bitcast.58, pred[8,256]{1,0:T(8,128)(4,1)S(1)} %fusion.68, f32[768]{0:T(1024)S(1)} %mul.244, bf16[32,256]{1,0:T(8,128)(2,1)S(1)} %get-tuple-element.150), kind=kOutput, calls=%fused_computation.8.clone.1 | convolution fusion | flops 102629376 | bytes 3560960 | tf_op jit(solution)/shard_map/while/body/eval_jaxpr/qt,btx->bqx/dot_general | solution.py:70
  173.4 7.3 %reshape.250 = bf16[64,16,2,768]{3,2,1,0:T(2,128)(2,1)} reshape(bf16[8,8,32,768]{3,2,1,0:T(8,128)(2,1)} %get-tuple-element.39) | data formatting | bytes 6291456 | tf_op jit(solution)/shard_map/reshape | solution.py:74
  180.7 3.6 %copy.26 = bf16[16,2,64,768]{3,2,1,0:T(8,128)(2,1)S(1)} copy(bf16[16,2,64,768]{3,1,0,2:T(2,128)(2,1)} %bitcast.61) | data formatting | bytes 6291456 | tf_op jit(solution)/shard_map/transpose | solution.py:75
  184.3 1.0 fusion.55
  185.6 0.9 pad_maximum_fusion
  186.6 2.4 fusion.25
  188.9 5.3 %reduce-scatter.2.cloned.1.call-done = bf16[512,128]{1,0:T(8,128)(2,1)} async-done(((bf16[1024,128]{1,0:T(8,128)(2,1)}), bf16[512,128]{1,0:T(8,128)(2,1)}) %reduce-scatter.2.cloned.1.call-update) | async-done | bytes 131088 | tf_op jit(solution)/shard_map/reduce_scatter | solution.py:81
  194.2 80.0 %all-reduce.1 = f32[512,128]{1,0:T(8,128)S(1)} all-reduce(bf16[512,128]{1,0:T(8,128)(2,1)} %reduce-scatter.2.cloned.1.call-done), channel_id=1, replica_groups=mesh['sx'=16,'sy'=2] {'sx'}, use_global_device_ids=true, to_apply=%region_6.7 | all-reduce | flops 65536 | bytes 393216 | tf_op jit(solution)/shard_map/psum | solution.py:84
  275.1 1.7 copy.53
  277.6 2.0 multiply_reduce_fusion.3
  279.7 2.5 psum.23
  282.9 1.8 all_gather.3
  285.5 1.3 copy.31
  (91 shorter events, 11.9 us)
Async XLA Ops:
  7.2 179.4 %copy-start = (f32[16,64,2,8]{1,3,2,0:T(8,128)S(1)}, f32[16,64,2,8]{1,3,2,0:T(8,128)}, u32[]{:S(2)}) copy-start(f32[16,64,2,8]{1,3,2,0:T(8,128)} %param.9) | copy-start | bytes 196612
  7.2 6.2 %copy-start.1 = (bf16[1024,3,2,128]{3,2,1,0:T(2,128)(2,1)S(1)}, bf16[1024,3,2,128]{3,2,1,0:T(2,128)(2,1)}, u32[]{:S(2)}) copy-start(bf16[1024,3,2,128]{3,2,1,0:T(2,128)(2,1)} %param.7) | copy-start | bytes 4718596
  7.2 6.2 %copy-start.2 = (f32[3,2,128]{2,1,0:T(2,128)S(1)}, f32[3,2,128]{2,1,0:T(2,128)}, u32[]{:S(2)}) copy-start(f32[3,2,128]{2,1,0:T(2,128)} %param.8) | copy-start | bytes 9220
  7.2 50.9 %copy-start.3 = (s32[64]{0:T(128)S(1)}, s32[64]{0:T(128)}, u32[]{:S(2)}) copy-start(s32[64]{0:T(128)} %param.11) | copy-start | bytes 772
  7.2 187.0 %reduce-scatter.2.cloned.1.call-start = ((), (), s32[]{:S(2)}) async-start(), calls=%async_computation.1 | async-start | bytes 393216 | tf_op jit(solution)/shard_map/reduce_scatter | solution.py:81
Sparse Core Ops, SparseCore 0:
  186.6 7.5 reduce-scatter.1
where the time goes:
time: 295 us; the launch traced here: 294 us
  blocking collectives  126 us (43%)
  local copies, waits for them, and re-layouts  100 us (34%)
  matrix products  32.5 us (11%)
  between operations  14.9 us (5%)
  other arithmetic  9.15 us (3%)
  waiting for transfers between devices  5.29 us (2%)
  loops' own time  5.28 us (2%)
    psum x1, blocking collectives, shards(): owned = lax.psum(halves, 'sx') / denom  80 us
    gather x8, local copies, waits for them, and re-layouts, block_step(): windows = jnp.take(flat, times, axis=0)  75 us
    psum x1, blocking collectives, shards(): total_sq = lax.psum(local_sq, ('sx', 'sy'))  42.2 us
    dot_general x8, matrix products, block_step(): jnp.einsum('qt,btx->bqx', twid, windows, preferred_element_type=jnp.float32)  28.3 us
    reshape x1, local copies, waits for them, and re-layouts, shards(): blocks = blocks.reshape(nblock, nbins, 2, points)  7.28 us
  transfers between devices with their start and end apart: 1, of which 1 were waited for; matrix products, arithmetic and copies ran while one was open for 1% of the time, Pallas kernels for 0%

commit v1 on v0

v1 whole, which is shorter than its diff:
```python
import functools
import jax
import jax.numpy as jnp
from jax import lax
from jax.experimental import pallas as pl
from jax.experimental.pallas import tpu as pltpu
from jax.sharding import PartitionSpec as P

NFFT = 256
LANES = 128
EPS = 1e-06
MESH = pl.DeviceIdType.MESH


def make_twiddle(bins):
    steps = jnp.arange(NFFT, dtype=jnp.int32)
    window = 0.5 - 0.5 * jnp.cos(2.0 * jnp.pi * steps.astype(jnp.float32) / NFFT)
    norm_c = 1.0 / jnp.sqrt(jnp.sum(window * window))
    phase = bins[:, None] * steps[None, :] % NFFT
    angle = 2.0 * jnp.pi * phase.astype(jnp.float32) / NFFT
    twid = jnp.stack(
        [norm_c * window * jnp.cos(angle), -(norm_c * window) * jnp.sin(angle)], axis=1
    )
    return twid.astype(jnp.bfloat16)


def prep_kernel(dims, starts, x_ref, quad_ref, twid_ref, t_ref, xr_ref, sq_ref, xs):
    length, nvar, ctile, nblock, nq = dims
    rows = x_ref.shape[0]
    step = rows // 16

    @pl.loop(0, 16)
    def _(i):
        at = pl.ds(pl.multiple_of(i * step, step), step)
        xs[at, :] = x_ref[at, :].astype(jnp.float32)

    lane = lax.broadcasted_iota(jnp.int32, (1, LANES), 1)
    per_var = ctile // nvar
    total = jnp.zeros((1, LANES), jnp.float32)
    for c in range(ctile):
        col = xs[pl.ds(c, length, stride=ctile), :]
        xr_ref[:, c * LANES:(c + 1) * LANES] = col.astype(jnp.bfloat16)
        sums = jnp.sum(col * col, axis=0, keepdims=True) * quad_ref[c:c + 1, :]
        one = jnp.sum(sums, axis=1, keepdims=True)
        total = total + jnp.where(lane == c // per_var, one, 0.0)
    sq_ref[...] = total

    t_ref[...] = jnp.zeros_like(t_ref)
    tiles = NFFT // LANES
    wide = lax.broadcasted_iota(jnp.int32, (nq, LANES), 1)

    @pl.loop(0, nblock)
    def _(b):
        start = starts[b]
        tile = start // LANES
        shift = start - tile * LANES
        keep = wide < shift
        prev = jnp.zeros((nq, LANES), jnp.float32)
        outs = []
        for j in range(tiles):
            cur = pltpu.roll(twid_ref[:, j * LANES:(j + 1) * LANES], shift, 1)
            outs.append(jnp.where(keep, prev, cur))
            prev = cur
        outs.append(jnp.where(keep, prev, 0.0))
        t_ref[
            pl.ds(pl.multiple_of(b * nq, nq), nq),
            pl.ds(pl.multiple_of(tile * LANES, LANES), NFFT + LANES),
        ] = jnp.concatenate(outs, axis=1).astype(jnp.bfloat16)


def split2(value):
    high = value.astype(jnp.bfloat16)
    low = (value - high.astype(jnp.float32)).astype(jnp.bfloat16)
    return jnp.concatenate([high, low], axis=0)


def main_kernel(dims, t_ref, xr_ref, sq_ref, quad_ref, w_ref, modes_ref, energy_ref,
                qs, ys, sqbuf, zsend, zrecv, zall, sems):
    (length, nvar, ctile, nblock, nbins, nmode, n_x, n_y, per, grid_points) = dims
    n = n_x * n_y
    me = lax.axis_index("sx") * n_y + lax.axis_index("sy")

    def coords(k):
        t = lax.rem(me + k, n)
        return t, (t // n_y, lax.rem(t, n_y))

    barrier = pltpu.get_barrier_semaphore()

    def greet(k, carry):
        _, where = coords(k)
        pl.semaphore_signal(barrier, inc=1, device_id=where, device_id_type=MESH)
        return carry

    lax.fori_loop(1, n, greet, 0)
    pl.semaphore_wait(barrier, n - 1)

    def spread(src, dst, phase, by_target):
        def go(k, carry):
            t, where = coords(k)
            pltpu.make_async_remote_copy(
                src_ref=src.at[t] if by_target else src,
                dst_ref=dst.at[me],
                send_sem=sems.at[2 * phase],
                recv_sem=sems.at[2 * phase + 1],
                device_id=where,
                device_id_type=MESH,
            ).start()
            return carry

        lax.fori_loop(1, n, go, 0)

    def wait_all(dst, sem):
        rest = dst.at[pl.ds(0, n - 1)]
        pltpu.make_async_copy(rest, rest, sems.at[sem]).wait()

    spread(sq_ref, sqbuf, 0, False)

    nq = 2 * nbins
    chunk = nblock * nq // 4
    for j in range(ctile // 2):
        @pl.loop(0, 4)
        def _(i):
            at = pl.ds(pl.multiple_of(i * chunk, chunk), chunk)
            out = jnp.dot(
                t_ref[at, :length],
                xr_ref[:, 2 * j * LANES:2 * (j + 1) * LANES],
                preferred_element_type=jnp.float32,
            )
            qs[2 * j, at, :] = out[:, :LANES]
            qs[2 * j + 1, at, :] = out[:, LANES:]

    wait_all(sqbuf, 1)
    sqbuf[me] = sq_ref[...]
    total = jnp.sum(sqbuf[...], axis=0)
    scale = lax.rsqrt(total / (length * grid_points) + EPS)
    lane = lax.broadcasted_iota(jnp.int32, (1, LANES), 1)
    per_var = ctile // nvar
    cols = []
    for c in range(ctile):
        one = jnp.sum(jnp.where(lane == c // per_var, scale, 0.0), axis=1, keepdims=True)
        cols.append(one * jnp.sqrt(quad_ref[c:c + 1, :]))

    low_half = lax.broadcasted_iota(jnp.int32, (nmode, LANES), 1) < nblock
    pieces = nmode // per if per < nmode else 1
    for f in range(nbins):
        for c in range(ctile):
            for p in range(2):
                part = qs[c, pl.ds(2 * f + p, nblock, stride=nq), :]
                ys[f, p * nblock:(p + 1) * nblock, c * LANES:(c + 1) * LANES] = (
                    part * cols[c]
                ).astype(jnp.bfloat16)
        y = ys[f]
        u = jnp.dot(split2(w_ref[f]), y, preferred_element_type=jnp.float32)
        u = u[:2 * nmode] + u[2 * nmode:]
        a = lax.dot_general(
            split2(u), y, (((1,), (1,)), ((), ())), preferred_element_type=jnp.float32
        )
        a = (a[:2 * nmode] + a[2 * nmode:]) * (1.0 / (3.0 * grid_points))
        up = a[:nmode]
        z = pltpu.roll(a[nmode:], nblock, 1) + jnp.where(low_half, up, -up)
        for s in range(nmode // per):
            zsend[f * (nmode // per) + s] = z[s * per:(s + 1) * per]
    owners = nbins * nmode // per
    for s in range(owners, n):
        zsend[s] = jnp.zeros((per, LANES), jnp.float32)

    spread(zsend, zrecv, 1, True)
    wait_all(zrecv, 3)
    zrecv[me] = zsend[me]
    mine = jnp.sum(zrecv[...], axis=0)
    zall[me] = mine
    spread(zall.at[me], zall, 2, False)
    wait_all(zall, 5)
    wait_all(zrecv, 2)
    wait_all(zall, 4)
    wait_all(sqbuf, 0)

    for f in range(nbins):
        base = f * (nmode // per)
        z = jnp.concatenate([zall[base + s] for s in range(nmode // per)], axis=0)
        norms = jnp.sum(z * z, axis=1, keepdims=True)
        energy_ref[f] = jnp.broadcast_to(jnp.sqrt(norms / nblock), (nmode, LANES))
        coef = z * lax.rsqrt(norms + EPS)
        lhs = jnp.concatenate(
            [jnp.where(low_half, coef, -coef), pltpu.roll(coef, nblock, 1)], axis=0
        ).astype(jnp.bfloat16)
        m = jnp.dot(lhs, ys[f], preferred_element_type=jnp.float32)
        for c in range(ctile):
            modes_ref[pl.ds(f * 2 * nmode * ctile + c, 2 * nmode, stride=ctile), :] = (
                m[:, c * LANES:(c + 1) * LANES]
            )


def shards(n_x, n_y, snapshots, quad_weight, mode_guess, bins, starts):
    length, nvar, cols_x, cols_y = snapshots.shape
    nbins = bins.shape[0]
    nblock = starts.shape[0]
    nmode = mode_guess.shape[-1]
    ctile = nvar * cols_x
    points = ctile * cols_y
    nq = 2 * nbins
    n = n_x * n_y
    grid_points = cols_x * cols_y * n
    vmem = pl.BlockSpec(memory_space=pltpu.VMEM)
    smem = pl.BlockSpec(memory_space=pltpu.SMEM)
    limit = 60 * 1024 * 1024

    twid = make_twiddle(bins).reshape(nq, NFFT).astype(jnp.float32)
    x = snapshots.reshape(length * ctile, cols_y)
    quad = quad_weight.reshape(ctile, cols_y)
    guess_re = jnp.swapaxes(mode_guess[:, :, 0], 1, 2)
    guess_im = jnp.swapaxes(mode_guess[:, :, 1], 1, 2)
    w = jnp.concatenate(
        [
            jnp.concatenate([guess_re, -guess_im], axis=2),
            jnp.concatenate([guess_im, guess_re], axis=2),
        ],
        axis=1,
    )

    t, xr, sq = pl.pallas_call(
        functools.partial(prep_kernel, (length, nvar, ctile, nblock, nq)),
        name="prep",
        out_shape=(
            jax.ShapeDtypeStruct((nblock * nq, length + LANES), jnp.bfloat16),
            jax.ShapeDtypeStruct((length, points), jnp.bfloat16),
            jax.ShapeDtypeStruct((1, LANES), jnp.float32),
        ),
        in_specs=[smem, vmem, vmem, vmem],
        out_specs=(vmem, vmem, vmem),
        scratch_shapes=[pltpu.VMEM((length * ctile, cols_y), jnp.float32)],
        compiler_params=pltpu.CompilerParams(vmem_limit_bytes=limit // 2),
    )(starts, x, quad, twid)

    per = max(1, nbins * nmode // n)
    dims = (length, nvar, ctile, nblock, nbins, nmode, n_x, n_y, per, grid_points)
    modes, energy = pl.pallas_call(
        functools.partial(main_kernel, dims),
        name="spod",
        out_shape=(
            jax.ShapeDtypeStruct((nbins * 2 * nmode * ctile, cols_y), jnp.float32),
            jax.ShapeDtypeStruct((nbins, nmode, LANES), jnp.float32),
        ),
        in_specs=[vmem] * 5,
        out_specs=(vmem, vmem),
        scratch_shapes=[
            pltpu.VMEM((ctile, nblock * nq, LANES), jnp.float32),
            pltpu.VMEM((nbins, 2 * nblock, points), jnp.bfloat16),
            pltpu.VMEM((n, 1, LANES), jnp.float32),
            pltpu.VMEM((n, per, LANES), jnp.float32),
            pltpu.VMEM((n, per, LANES), jnp.float32),
            pltpu.VMEM((n, per, LANES), jnp.float32),
            pltpu.SemaphoreType.DMA((6,)),
        ],
        compiler_params=pltpu.CompilerParams(
            collective_id=0, has_side_effects=True, vmem_limit_bytes=limit // 2
        ),
    )(t, xr, sq, quad, w)
    return (
        modes.reshape(nbins, 2, nmode, nvar, cols_x, cols_y),
        energy[:, :, 0],
    )


def solution(mesh):
    n_x, n_y = mesh.shape["sx"], mesh.shape["sy"]
    return jax.shard_map(
        functools.partial(shards, n_x, n_y),
        mesh=mesh,
        in_specs=(P(None, None, "sx", "sy"), P(None, "sx", "sy"), P(), P(), P()),
        out_specs=(P(None, None, None, None, "sx", "sy"), P()),
        check_vma=False,
    )
```

time: 295 us -> 44.7 us (0.15)
  blocking collectives: 126 us -> 0 us
  local copies, waits for them, and re-layouts: 100 us -> 5.28 us
  Pallas kernels: 0 us -> 35.3 us
  matrix products: 32.5 us -> 0 us
  between operations: 14.9 us -> 1.37 us
  other arithmetic: 9.15 us -> 2.46 us
  waiting for transfers between devices: 5.29 us -> 0 us
  loops' own time: 5.28 us -> 0 us
    psum x3 -> x0, blocking collectives: 125 us -> none  [the longest x1 80 us: shards(): owned = lax.psum(halves, 'sx') / denom]
    gather x8 -> x0, local copies, waits for them, and re-layouts: 75 us -> none  [block_step(): windows = jnp.take(flat, times, axis=0)]
    pallas_call x0 -> x2, Pallas kernels: none -> 35.3 us  [the longest x1 28.8 us: shards(): pl.pallas_call(functools.partial(main_kernel, dims), name='spod', out_sha...]
    dot_general x13 -> x0, matrix products: 32.5 us -> none  [the longest x8 28.3 us: block_step(): jnp.einsum('qt,btx->bqx', twid, windows, preferred_element_type=jnp.float32)]
    reshape x4 -> x1, local copies, waits for them, and re-layouts: 11.3 us -> 0.7 us  [shards(): quad = quad_weight.reshape(ctile, cols_y)]
    another operation x1 -> x0, loops' own time: 5.28 us -> none  [shards(): blocks = lax.map(block_step, jnp.arange(nblock // group, dtype=jnp.int32))]
    dynamic_slice x16 -> x0, local copies, waits for them, and re-layouts: 5.28 us -> none  [the longest x8 4.67 us: shards(): blocks = lax.map(block_step, jnp.arange(nblock // group, dtype=jnp.int32))]
    reduce_scatter x1 -> x0, waiting for transfers between devices: 5.27 us -> none  [shards(): lax.psum_scatter(local_gram.astype(jnp.bfloat16), 'sy', scatter_dimension...]
  transfers between devices with their start and end apart: 1 -> 0, of which waited for: 1 -> 0; matrix products, arithmetic and copies ran while one was open for 1% -> 0% of each run, Pallas kernels for 0% -> 0%
where the time goes in v1:
time: 44.7 us; the launch traced here: 44.4 us
  Pallas kernels  35.3 us (79%)
  local copies, waits for them, and re-layouts  5.28 us (12%)
  other arithmetic  2.46 us (6%)
  between operations  1.37 us (3%)
    pallas_call x1, Pallas kernels, shards(): pl.pallas_call(functools.partial(main_kernel, dims), name='spod', out_sha...  28.8 us
    pallas_call x1, Pallas kernels, shards(): pl.pallas_call(functools.partial(prep_kernel, (length, nvar, ctile, nbloc...  6.52 us
    unnamed x5, local copies, waits for them, and re-layouts  2.94 us

profile of v1, /device:TPU:0, one launch (start us, length us, event | category | flops | bytes accessed | tf_op | source)
XLA Modules:
  0.0 44.4 jit_solution(11648108526339003163)
XLA Ops:
  0.6 0.6 %multiply_reduce_fusion = f32[]{:T(128)} fusion(), kind=kLoop, calls=%fused_computation.15 | loop fusion | flops 1535 | bytes 4 | tf_op jit(solution)/shard_map/reduce_sum | solution.py:18
  2.0 0.7 %reshape.164.quad_ref = f32[6,128]{1,0:T(8,128)S(1)} reshape(f32[3,2,128]{2,1,0:T(2,128)} %param.6) | data formatting | bytes 6144 | tf_op jit(solution)/shard_map/reshape | solution.py:210
  2.7 0.8 %multiply_convert_fusion.1 = (bf16[16,1,256]{2,0,1:T(8,128)(2,1)S(1)}, bf16[16,1,256]{2,0,1:T(8,128)(2,1)S(1)}) fusion(s32[16]{0:T(128)} %param.8, f32[256]{0:T(256)S(1)} %get-tuple-element.16, f32[256]{0:T(256)S(1)} %get-tuple-element.17), kind=kLoop, calls=%fused_computation.11 | loop fusion | flops 73728 | bytes 18496 | tf_op jit(solution)/shard_map/convert.1
  3.6 0.8 %fusion.8 = f32[16,8,64]{2,1,0:T(8,128)S(1)} fusion(f32[16,64,2,8]{1,3,2,0:T(8,128)} %param.7), kind=kLoop, calls=%fused_computation.19 | loop fusion | flops 8192 | bytes 65536 | tf_op jit(solution)/shard_map/neg | solution.py:215
  4.4 0.9 %slice_bitcast_fusion = (f32[16,8,64]{2,1,0:T(8,128)S(1)}, f32[16,8,64]{2,1,0:T(8,128)S(1)}) fusion(f32[16,64,2,8]{1,3,2,0:T(8,128)} %param.7), kind=kLoop, calls=%fused_computation.1 | loop fusion | bytes 131072 | tf_op jit(solution)/shard_map/transpose | solution.py:212
  5.3 0.1 maximum_maximum_fusion.w_ref
  5.4 0.0 copy-start
  5.5 1.4 %copy-done = bf16[1024,3,2,128]{3,2,1,0:T(2,128)(2,1)S(1)} copy-done((bf16[1024,3,2,128]{3,2,1,0:T(2,128)(2,1)S(1)}, bf16[1024,3,2,128]{3,2,1,0:T(2,128)(2,1)}, u32[]{:S(2)}) %copy-start) | copy-done | bytes 1572888
  6.9 0.0 copy-start.1
  6.9 0.7 %copy-done.1 = s32[64]{0:T(128)S(1)} copy-done((s32[64]{0:T(128)S(1)}, s32[64]{0:T(128)}, u32[]{:S(2)}) %copy-start.1) | copy-done | bytes 280
  7.5 6.5 %prep.1 = (bf16[2048,1152]{1,0:T(8,128)(2,1)S(1)}, bf16[1024,768]{1,0:T(8,128)(2,1)S(1)}, f32[1,128]{1,0:T(1,128)S(1)}) custom-call(s32[64]{0:T(128)S(1)} %copy-done.1, bf16[6144,128]{1,0:T(8,128)(2,1)S(1)} %bitcast.18, f32[6,128]{1,0:T(8,128)S(1)} %reshape.164.quad_ref, f32[32,256]{1,0:T(8,128)S(1)} %reshape.166.twid_ref), custom_call_target="tpu_custom_call" | custom-call | tf_op jit(solution)/shard_map/prep/pallas_call | solution.py:221
  14.0 28.8 %spod.1 = (f32[1536,128]{1,0:T(8,128)S(1)}, f32[16,8,128]{2,1,0:T(8,128)S(1)}) custom-call(bf16[2048,1152]{1,0:T(8,128)(2,1)S(1)} %get-tuple-element.7.t_ref, bf16[1024,768]{1,0:T(8,128)(2,1)S(1)} %get-tuple-element.8.xr_ref, f32[1,128]{1,0:T(1,128)S(1)} %get-tuple-element.9.sq_ref, f32[6,128]{1,0:T(8,128)S(1)} %reshape.164.quad_ref, ...), custom_call_target="tpu_custom_call" | custom-call | tf_op jit(solution)/shard_map/spod/pallas_call | solution.py:237
  42.8 0.7 %copy.13 = f32[16,8,1]{0,1,2:T(8,128)} copy(f32[16,8,1]{2,1,0:T(8,128)S(1)} %bitcast.20) | data formatting | bytes 1024 | tf_op jit(solution)/shard_map/slice | solution.py:261
  43.5 0.9 %copy.17 = f32[16,2,8,3,2,128]{5,4,3,2,1,0:T(2,128)} copy(f32[16,2,8,3,2,128]{5,4,3,2,1,0:T(2,128)S(1)} %bitcast.19) | data formatting | bytes 1572864
  (4 shorter events, 0.1 us)
Async XLA Ops:
  5.4 1.4 %copy-start = (bf16[1024,3,2,128]{3,2,1,0:T(2,128)(2,1)S(1)}, bf16[1024,3,2,128]{3,2,1,0:T(2,128)(2,1)}, u32[]{:S(2)}) copy-start(bf16[1024,3,2,128]{3,2,1,0:T(2,128)(2,1)} %param.5) | copy-start | bytes 4718596
  6.9 0.7 %copy-start.1 = (s32[64]{0:T(128)S(1)}, s32[64]{0:T(128)}, u32[]{:S(2)}) copy-start(s32[64]{0:T(128)} %starts.1) | copy-start | bytes 772

commit v2 on v1

v2 whole, which is shorter than its diff:
```python
import functools
import jax
import jax.numpy as jnp
from jax import lax
from jax.experimental import pallas as pl
from jax.experimental.pallas import tpu as pltpu
from jax.sharding import PartitionSpec as P

NFFT = 256
LANES = 128
EPS = 1e-06
MESH = pl.DeviceIdType.MESH


def twiddle_kernel(dims, starts, bins, t_ref, tw):
    nblock, nbins = dims
    nq = 2 * nbins

    shape = (nbins, NFFT)
    row = lax.broadcasted_iota(jnp.int32, shape, 0)
    step = lax.broadcasted_iota(jnp.int32, shape, 1)
    number = jnp.zeros(shape, jnp.int32)
    for f in range(nbins):
        number = jnp.where(row == f, bins[f], number)
    turn = 2.0 * jnp.pi / NFFT
    window = 0.5 - 0.5 * jnp.cos(step.astype(jnp.float32) * turn)
    norm_c = lax.rsqrt(jnp.sum(window * window, axis=1, keepdims=True))
    phase = lax.rem(number * step, NFFT)
    angle = phase.astype(jnp.float32) * turn
    tw[:nbins, :] = norm_c * window * jnp.cos(angle)
    tw[nbins:, :] = -(norm_c * window) * jnp.sin(angle)

    tiles = NFFT // LANES
    wide = lax.broadcasted_iota(jnp.int32, (nq, LANES), 1)
    t_ref[...] = jnp.zeros_like(t_ref)

    def place(b, carry):
        start = starts[b]
        tile = start // LANES
        shift = start - tile * LANES
        keep = wide < shift
        prev = jnp.zeros((nq, LANES), jnp.float32)
        outs = []
        for j in range(tiles):
            cur = pltpu.roll(tw[:, j * LANES:(j + 1) * LANES], shift, 1)
            outs.append(jnp.where(keep, prev, cur))
            prev = cur
        outs.append(jnp.where(keep, prev, 0.0))
        t_ref[
            pl.ds(pl.multiple_of(b * nq, nq), nq),
            pl.ds(pl.multiple_of(tile * LANES, LANES), NFFT + LANES),
        ] = jnp.concatenate(outs, axis=1).astype(jnp.bfloat16)
        return carry

    lax.fori_loop(0, nblock, place, 0, unroll=4)


def split2(value):
    high = value.astype(jnp.bfloat16)
    low = (value - high.astype(jnp.float32)).astype(jnp.bfloat16)
    return jnp.concatenate([high, low], axis=0)


def main_kernel(dims, t_ref, x_ref, quad_ref, guess_ref, y_ref, z_ref,
                xs, xr, sq, qs, sqbuf, zsend, zrecv, zall, sems):
    (length, nvar, ctile, nblock, nbins, nmode, n_x, n_y, per, grid_points) = dims
    n = n_x * n_y
    me = lax.axis_index("sx") * n_y + lax.axis_index("sy")
    per_var = ctile // nvar

    def coords(k):
        t = lax.rem(me + k, n)
        return t, (t // n_y, lax.rem(t, n_y))

    barrier = pltpu.get_barrier_semaphore()

    def greet(k, carry):
        _, where = coords(k)
        pl.semaphore_signal(barrier, inc=1, device_id=where, device_id_type=MESH)
        return carry

    lax.fori_loop(1, n, greet, 0)

    def spread(src, dst, phase, by_target):
        def go(k, carry):
            t, where = coords(k)
            pltpu.make_async_remote_copy(
                src_ref=src.at[t] if by_target else src,
                dst_ref=dst.at[me],
                send_sem=sems.at[2 * phase],
                recv_sem=sems.at[2 * phase + 1],
                device_id=where,
                device_id_type=MESH,
            ).start()
            return carry

        lax.fori_loop(1, n, go, 0)

    def wait_all(dst, sem):
        rest = dst.at[pl.ds(0, n - 1)]
        pltpu.make_async_copy(rest, rest, sems.at[sem]).wait()

    rows = x_ref.shape[0]
    step = rows // 16

    @pl.loop(0, 16)
    def _(i):
        at = pl.ds(pl.multiple_of(i * step, step), step)
        xs[at, :] = x_ref[at, :].astype(jnp.float32)

    lane = lax.broadcasted_iota(jnp.int32, (1, LANES), 1)
    quads = [quad_ref[c // per_var, c % per_var:c % per_var + 1, :] for c in range(ctile)]
    total = jnp.zeros((1, LANES), jnp.float32)
    for c in range(ctile):
        col = xs[pl.ds(c, length, stride=ctile), :]
        xr[:, c * LANES:(c + 1) * LANES] = col.astype(jnp.bfloat16)
        sums = jnp.sum(col * col, axis=0, keepdims=True) * quads[c]
        one = jnp.sum(sums, axis=1, keepdims=True)
        total = total + jnp.where(lane == c // per_var, one, 0.0)
    sq[...] = total

    pl.semaphore_wait(barrier, n - 1)
    spread(sq, sqbuf, 0, False)

    nq = 2 * nbins
    chunk = nblock * nq // 4
    for j in range(ctile // 2):
        @pl.loop(0, 4)
        def _(i):
            at = pl.ds(pl.multiple_of(i * chunk, chunk), chunk)
            out = jnp.dot(
                t_ref[at, :length],
                xr[:, 2 * j * LANES:2 * (j + 1) * LANES],
                preferred_element_type=jnp.float32,
            )
            qs[2 * j, at, :] = out[:, :LANES]
            qs[2 * j + 1, at, :] = out[:, LANES:]

    wait_all(sqbuf, 1)
    sqbuf[me] = sq[...]
    total = jnp.sum(sqbuf[...], axis=0)
    scale = lax.rsqrt(total / (length * grid_points) + EPS)
    cols = []
    for c in range(ctile):
        one = jnp.sum(jnp.where(lane == c // per_var, scale, 0.0), axis=1, keepdims=True)
        cols.append(one * jnp.sqrt(quads[c]))

    low_half = lax.broadcasted_iota(jnp.int32, (nmode, LANES), 1) < nblock
    parts = nmode // per
    for f in range(nbins):
        for c in range(ctile):
            for p in range(2):
                part = qs[c, pl.ds(p * nbins + f, nblock, stride=nq), :]
                y_ref[f, p * nblock:(p + 1) * nblock, c * LANES:(c + 1) * LANES] = (
                    part * cols[c]
                ).astype(jnp.bfloat16)
        y = y_ref[f]
        g_re, g_im = guess_ref[f, 0], guess_ref[f, 1]
        w = jnp.concatenate(
            [
                jnp.concatenate([g_re, -g_im], axis=1),
                jnp.concatenate([g_im, g_re], axis=1),
            ],
            axis=0,
        )
        u = jnp.dot(split2(w), y, preferred_element_type=jnp.float32)
        u = u[:2 * nmode] + u[2 * nmode:]
        a = lax.dot_general(
            split2(u), y, (((1,), (1,)), ((), ())), preferred_element_type=jnp.float32
        )
        a = (a[:2 * nmode] + a[2 * nmode:]) * (1.0 / (3.0 * grid_points))
        up = a[:nmode]
        z = pltpu.roll(a[nmode:], nblock, 1) + jnp.where(low_half, up, -up)
        for s in range(parts):
            zsend[f * parts + s] = z[s * per:(s + 1) * per]
    owners = nbins * parts
    for s in range(owners, n):
        zsend[s] = jnp.zeros((per, LANES), jnp.float32)

    spread(zsend, zrecv, 1, True)
    wait_all(zrecv, 3)
    zrecv[me] = zsend[me]
    zall[me] = jnp.sum(zrecv[...], axis=0)
    spread(zall.at[me], zall, 2, False)
    wait_all(zall, 5)
    for s in range(owners):
        z_ref[s * per:(s + 1) * per] = zall[s]
    wait_all(zrecv, 2)
    wait_all(zall, 4)
    wait_all(sqbuf, 0)


def modes_kernel(dims, y_ref, z_ref, modes_hbm, energy_ref, out, sems):
    ctile, nblock, nbins, nmode = dims
    span = 2 * nmode * ctile
    low_half = lax.broadcasted_iota(jnp.int32, (nmode, LANES), 1) < nblock
    column = lax.broadcasted_iota(jnp.int32, (nmode, nbins), 1)
    energy = jnp.zeros((nmode, nbins), jnp.float32)

    def store(f):
        at = pl.ds(f * span, span)
        return pltpu.make_async_copy(out.at[at], modes_hbm.at[at], sems.at[f])

    for f in range(nbins):
        z = z_ref[f * nmode:(f + 1) * nmode]
        norms = jnp.sum(z * z, axis=1, keepdims=True)
        energy = jnp.where(column == f, jnp.sqrt(norms / nblock), energy)
        coef = z * lax.rsqrt(norms + EPS)
        lhs = jnp.concatenate(
            [jnp.where(low_half, coef, -coef), pltpu.roll(coef, nblock, 1)], axis=0
        ).astype(jnp.bfloat16)
        m = jnp.dot(lhs, y_ref[f], preferred_element_type=jnp.float32)
        for c in range(ctile):
            out[pl.ds(f * span + c, 2 * nmode, stride=ctile), :] = (
                m[:, c * LANES:(c + 1) * LANES]
            )
        if f > 0:
            store(f - 1).start()
    energy_ref[...] = energy
    store(nbins - 1).start()
    for f in range(nbins):
        store(f).wait()


def shards(n_x, n_y, snapshots, quad_weight, mode_guess, bins, starts):
    length, nvar, cols_x, cols_y = snapshots.shape
    nbins = bins.shape[0]
    nblock = starts.shape[0]
    nmode = mode_guess.shape[-1]
    ctile = nvar * cols_x
    points = ctile * cols_y
    nq = 2 * nbins
    n = n_x * n_y
    grid_points = cols_x * cols_y * n
    vmem = pl.BlockSpec(memory_space=pltpu.VMEM)
    smem = pl.BlockSpec(memory_space=pltpu.SMEM)
    hbm = pl.BlockSpec(memory_space=pltpu.HBM)
    limit = 30 * 1024 * 1024

    x = snapshots.reshape(length * ctile, cols_y)
    guess = jnp.transpose(mode_guess, (0, 2, 3, 1))

    t = pl.pallas_call(
        functools.partial(twiddle_kernel, (nblock, nbins)),
        name="twiddle",
        out_shape=jax.ShapeDtypeStruct((nblock * nq, length + LANES), jnp.bfloat16),
        in_specs=[smem, smem],
        out_specs=vmem,
        scratch_shapes=[pltpu.VMEM((nq, NFFT), jnp.float32)],
        compiler_params=pltpu.CompilerParams(vmem_limit_bytes=limit),
        cost_estimate=pl.CostEstimate(
            flops=0, transcendentals=0, bytes_accessed=2 * nblock * nq * (length + LANES)
        ),
    )(starts, bins)

    per = max(1, nbins * nmode // n)
    dims = (length, nvar, ctile, nblock, nbins, nmode, n_x, n_y, per, grid_points)
    y, z = pl.pallas_call(
        functools.partial(main_kernel, dims),
        name="spod",
        out_shape=(
            jax.ShapeDtypeStruct((nbins, 2 * nblock, points), jnp.bfloat16),
            jax.ShapeDtypeStruct((nbins * nmode, LANES), jnp.float32),
        ),
        in_specs=[vmem] * 4,
        out_specs=(vmem, vmem),
        scratch_shapes=[
            pltpu.VMEM((length * ctile, cols_y), jnp.float32),
            pltpu.VMEM((length, points), jnp.bfloat16),
            pltpu.VMEM((1, LANES), jnp.float32),
            pltpu.VMEM((ctile, nblock * nq, LANES), jnp.float32),
            pltpu.VMEM((n, 1, LANES), jnp.float32),
            pltpu.VMEM((n, per, LANES), jnp.float32),
            pltpu.VMEM((n, per, LANES), jnp.float32),
            pltpu.VMEM((n, per, LANES), jnp.float32),
            pltpu.SemaphoreType.DMA((6,)),
        ],
        compiler_params=pltpu.CompilerParams(
            collective_id=0, has_side_effects=True, vmem_limit_bytes=limit
        ),
    )(t, x, quad_weight, guess)

    modes, energy = pl.pallas_call(
        functools.partial(modes_kernel, (ctile, nblock, nbins, nmode)),
        name="modes",
        out_shape=(
            jax.ShapeDtypeStruct((nbins * 2 * nmode * ctile, cols_y), jnp.float32),
            jax.ShapeDtypeStruct((nmode, nbins), jnp.float32),
        ),
        in_specs=[vmem, vmem],
        out_specs=(hbm, vmem),
        scratch_shapes=[
            pltpu.VMEM((nbins * 2 * nmode * ctile, cols_y), jnp.float32),
            pltpu.SemaphoreType.DMA((nbins,)),
        ],
        compiler_params=pltpu.CompilerParams(vmem_limit_bytes=limit),
    )(y, z)
    return (
        modes.reshape(nbins, 2, nmode, nvar, cols_x, cols_y),
        energy.T,
    )


def solution(mesh):
    n_x, n_y = mesh.shape["sx"], mesh.shape["sy"]
    return jax.shard_map(
        functools.partial(shards, n_x, n_y),
        mesh=mesh,
        in_specs=(P(None, None, "sx", "sy"), P(None, "sx", "sy"), P(), P(), P()),
        out_specs=(P(None, None, None, None, "sx", "sy"), P()),
        check_vma=False,
    )
```

time: 44.7 us -> 34.4 us (0.77)
  local copies, waits for them, and re-layouts: 5.28 us -> 1.44 us
  Pallas kernels: 35.3 us -> 32.1 us
  other arithmetic: 2.46 us -> 0 us
  between operations: 1.37 us -> 0.7 us
    pallas_call x1, Pallas kernels: 28.8 us -> 27.1 us  [shards(): pl.pallas_call(functools.partial(main_kernel, dims), name='spod', out_sha...]
    pallas_call x1 -> x2, Pallas kernels: 6.52 us -> 4.93 us  [the longest x1 2.54 us: shards(): pl.pallas_call(functools.partial(twiddle_kernel, (nblock, nbins)), name='...]
    unnamed x5 -> x10, local copies, waits for them, and re-layouts: 2.94 us -> 1.44 us
    transpose x1 -> x0, local copies, waits for them, and re-layouts: 0.88 us -> none  [shards(): guess_im = jnp.swapaxes(mode_guess[:, :, 1], 1, 2)]
    neg x1 -> x0, other arithmetic: 0.85 us -> none  [shards(): -guess_im]
    another operation x1 -> x0, other arithmetic: 0.81 us -> none
    slice x1 -> x0, local copies, waits for them, and re-layouts: 0.72 us -> none  [shards(): energy[:, :, 0]]
    reshape x1 -> x0, local copies, waits for them, and re-layouts: 0.7 us -> none  [shards(): quad = quad_weight.reshape(ctile, cols_y)]
where the time goes in v2:
time: 34.4 us; the launch traced here: 34.2 us
  Pallas kernels  32.1 us (93%)
  local copies, waits for them, and re-layouts  1.44 us (4%)
  between operations  0.7 us (2%)
    pallas_call x1, Pallas kernels, shards(): pl.pallas_call(functools.partial(main_kernel, dims), name='spod', out_sha...  27.1 us
    pallas_call x1, Pallas kernels, shards(): pl.pallas_call(functools.partial(twiddle_kernel, (nblock, nbins)), name='...  2.54 us
    pallas_call x1, Pallas kernels, shards(): pl.pallas_call(functools.partial(modes_kernel, (ctile, nblock, nbins, nmo...  2.39 us
    unnamed x10, local copies, waits for them, and re-layouts  1.44 us

profile of v2, /device:TPU:0, one launch (start us, length us, event | category | flops | bytes accessed | tf_op | source)
XLA Modules:
  0.0 34.2 jit_solution(14362781793007040987)
XLA Ops:
  0.6 0.0 copy-start.1
  0.6 0.0 copy-start.2
  0.7 0.0 copy-start
  0.7 0.0 copy-start.3
  0.7 0.8 %copy-done.3 = s32[64]{0:T(128)S(1)} copy-done((s32[64]{0:T(128)S(1)}, s32[64]{0:T(128)}, u32[]{:S(2)}) %copy-start.3) | copy-done | bytes 280
  1.4 0.0 copy-start.4
  1.4 0.7 %copy-done.4 = s32[16]{0:T(128)S(1)} copy-done((s32[16]{0:T(128)S(1)}, s32[16]{0:T(128)}, u32[]{:S(2)}) %copy-start.4) | copy-done | bytes 88
  2.1 2.5 %twiddle.1.t_ref = bf16[2048,1152]{1,0:T(8,128)(2,1)S(1)} custom-call(s32[64]{0:T(128)S(1)} %copy-done.3, s32[16]{0:T(128)S(1)} %copy-done.4), custom_call_target="tpu_custom_call" | custom-call | bytes 4718592 | tf_op jit(solution)/shard_map/twiddle/pallas_call | solution.py:243
  4.6 0.0 copy-done.1
  4.7 0.0 copy-done.2
  4.7 0.0 copy-done
  4.7 27.1 %spod.1 = (bf16[16,128,768]{2,1,0:T(8,128)(2,1)S(1)}, f32[128,128]{1,0:T(8,128)S(1)}) custom-call(bf16[2048,1152]{1,0:T(8,128)(2,1)S(1)} %twiddle.1.t_ref, bf16[6144,128]{1,0:T(8,128)(2,1)S(1)} %bitcast.4, f32[3,2,128]{2,1,0:T(2,128)S(1)} %copy-done.2, f32[16,2,8,64]{3,2,1,0:T(8,128)S(1)} %bitcast.5), custom_call_target="tpu_custom_call" | custom-call | tf_op jit(solution)/shard_map/spod/pallas_call | solution.py:258
  31.8 2.4 %modes.1 = (f32[1536,128]{1,0:T(8,128)}, f32[8,16]{1,0:T(8,128)}) custom-call(bf16[16,128,768]{2,1,0:T(8,128)(2,1)S(1)} %get-tuple-element.6.y_ref, f32[128,128]{1,0:T(8,128)S(1)} %get-tuple-element.7.z_ref), custom_call_target="tpu_custom_call" | custom-call | tf_op jit(solution)/shard_map/modes/pallas_call | solution.py:283
Async XLA Ops:
  0.6 4.0 %copy-start.1 = (f32[16,64,2,8]{1,3,2,0:T(8,128)S(1)}, f32[16,64,2,8]{1,3,2,0:T(8,128)}, u32[]{:S(2)}) copy-start(f32[16,64,2,8]{1,3,2,0:T(8,128)} %param.7) | copy-start | bytes 196612
  0.6 4.0 %copy-start.2 = (f32[3,2,128]{2,1,0:T(2,128)S(1)}, f32[3,2,128]{2,1,0:T(2,128)}, u32[]{:S(2)}) copy-start(f32[3,2,128]{2,1,0:T(2,128)} %quad_ref.1) | copy-start | bytes 9220
  0.7 4.0 %copy-start = (bf16[1024,3,2,128]{3,2,1,0:T(2,128)(2,1)S(1)}, bf16[1024,3,2,128]{3,2,1,0:T(2,128)(2,1)}, u32[]{:S(2)}) copy-start(bf16[1024,3,2,128]{3,2,1,0:T(2,128)(2,1)} %param.5) | copy-start | bytes 4718596
  0.7 0.8 %copy-start.3 = (s32[64]{0:T(128)S(1)}, s32[64]{0:T(128)}, u32[]{:S(2)}) copy-start(s32[64]{0:T(128)} %starts.1) | copy-start | bytes 772
  1.4 0.7 %copy-start.4 = (s32[16]{0:T(128)S(1)}, s32[16]{0:T(128)}, u32[]{:S(2)}) copy-start(s32[16]{0:T(128)} %bins.1) | copy-start | bytes 196

commit v3 on v2

--- a/solution.py
+++ b/solution.py
@@ -12,10 +12,7 @@
 MESH = pl.DeviceIdType.MESH
 
 
-def twiddle_kernel(dims, starts, bins, t_ref, tw):
-    nblock, nbins = dims
-    nq = 2 * nbins
-
+def fill_twiddle(bins, nbins, tw):
     shape = (nbins, NFFT)
     row = lax.broadcasted_iota(jnp.int32, shape, 0)
     step = lax.broadcasted_iota(jnp.int32, shape, 1)
@@ -30,29 +27,26 @@
     tw[:nbins, :] = norm_c * window * jnp.cos(angle)
     tw[nbins:, :] = -(norm_c * window) * jnp.sin(angle)
 
-    tiles = NFFT // LANES
+
+def shifted_rows(start, nq, length, tw):
+    tile = start // LANES
+    shift = start - tile * LANES
     wide = lax.broadcasted_iota(jnp.int32, (nq, LANES), 1)
-    t_ref[...] = jnp.zeros_like(t_ref)
-
-    def place(b, carry):
-        start = starts[b]
-        tile = start // LANES
-        shift = start - tile * LANES
-        keep = wide < shift
-        prev = jnp.zeros((nq, LANES), jnp.float32)
-        outs = []
-        for j in range(tiles):
-            cur = pltpu.roll(tw[:, j * LANES:(j + 1) * LANES], shift, 1)
-            outs.append(jnp.where(keep, prev, cur))
-            prev = cur
-        outs.append(jnp.where(keep, prev, 0.0))
-        t_ref[
-            pl.ds(pl.multiple_of(b * nq, nq), nq),
-            pl.ds(pl.multiple_of(tile * LANES, LANES), NFFT + LANES),
-        ] = jnp.concatenate(outs, axis=1).astype(jnp.bfloat16)
-        return carry
-
-    lax.fori_loop(0, nblock, place, 0, unroll=4)
+    keep = wide < shift
+    zero = jnp.zeros((nq, LANES), jnp.float32)
+    prev, pieces = zero, []
+    for j in range(NFFT // LANES):
+        cur = pltpu.roll(tw[:, j * LANES:(j + 1) * LANES], shift, 1)
+        pieces.append(jnp.where(keep, prev, cur))
+        prev = cur
+    pieces.append(jnp.where(keep, prev, zero))
+    outs = []
+    for j in range(length // LANES):
+        out = zero
+        for i, piece in enumerate(pieces):
+            out = jnp.where(tile + i == j, piece, out)
+        outs.append(out)
+    return jnp.concatenate(outs, axis=1).astype(jnp.bfloat16)
 
 
 def split2(value):
@@ -61,12 +55,28 @@
     return jnp.concatenate([high, low], axis=0)
 
 
-def main_kernel(dims, t_ref, x_ref, quad_ref, guess_ref, y_ref, z_ref,
-                xs, xr, sq, qs, sqbuf, zsend, zrecv, zall, sems):
+def main_kernel(dims, starts_hbm, bins_hbm, x_hbm, quad_hbm, guess_hbm, y_ref, z_ref,
+                starts, bins, x_ref, quad_ref, guess_ref, t_ref, tw, xs, xr, sq, qs,
+                sqbuf, zsend, zrecv, zall, load_sems, sems):
     (length, nvar, ctile, nblock, nbins, nmode, n_x, n_y, per, grid_points) = dims
     n = n_x * n_y
     me = lax.axis_index("sx") * n_y + lax.axis_index("sy")
     per_var = ctile // nvar
+    nq = 2 * nbins
+    loads = [
+        pltpu.make_async_copy(src, dst, load_sems.at[i])
+        for i, (src, dst) in enumerate(
+            [
+                (bins_hbm, bins),
+                (starts_hbm, starts),
+                (quad_hbm, quad_ref),
+                (x_hbm, x_ref),
+                (guess_hbm, guess_ref),
+            ]
+        )
+    ]
+    for load in loads:
+        load.start()
 
     def coords(k):
         t = lax.rem(me + k, n)
@@ -100,6 +110,10 @@
         rest = dst.at[pl.ds(0, n - 1)]
         pltpu.make_async_copy(rest, rest, sems.at[sem]).wait()
 
+    loads[0].wait()
+    fill_twiddle(bins, nbins, tw)
+    for load in loads[1:]:
+        load.wait()
     rows = x_ref.shape[0]
     step = rows // 16
 
@@ -122,14 +136,21 @@
     pl.semaphore_wait(barrier, n - 1)
     spread(sq, sqbuf, 0, False)
 
-    nq = 2 * nbins
+    @pl.loop(0, nblock // 4)
+    def _(i):
+        for k in range(4):
+            b = i * 4 + k
+            t_ref[pl.ds(pl.multiple_of(b * nq, nq), nq), :] = shifted_rows(
+                starts[b], nq, length, tw
+            )
+
     chunk = nblock * nq // 4
     for j in range(ctile // 2):
         @pl.loop(0, 4)
         def _(i):
             at = pl.ds(pl.multiple_of(i * chunk, chunk), chunk)
             out = jnp.dot(
-                t_ref[at, :length],
+                t_ref[at, :],
                 xr[:, 2 * j * LANES:2 * (j + 1) * LANES],
                 preferred_element_type=jnp.float32,
             )
@@ -233,26 +254,16 @@
     n = n_x * n_y
     grid_points = cols_x * cols_y * n
     vmem = pl.BlockSpec(memory_space=pltpu.VMEM)
-    smem = pl.BlockSpec(memory_space=pltpu.SMEM)
     hbm = pl.BlockSpec(memory_space=pltpu.HBM)
     limit = 30 * 1024 * 1024
 
     x = snapshots.reshape(length * ctile, cols_y)
     guess = jnp.transpose(mode_guess, (0, 2, 3, 1))
 
-    t = pl.pallas_call(
-        functools.partial(twiddle_kernel, (nblock, nbins)),
-        name="twiddle",
-        out_shape=jax.ShapeDtypeStruct((nblock * nq, length + LANES), jnp.bfloat16),
-        in_specs=[smem, smem],
-        out_specs=vmem,
-        scratch_shapes=[pltpu.VMEM((nq, NFFT), jnp.float32)],
-        compiler_params=pltpu.CompilerParams(vmem_limit_bytes=limit),
-        cost_estimate=pl.CostEstimate(
-            flops=0, transcendentals=0, bytes_accessed=2 * nblock * nq * (length + LANES)
-        ),
-    )(starts, bins)
-
+    operands = [
+        pltpu.with_memory_space_constraint(value, pltpu.HBM)
+        for value in (starts, bins, x, quad_weight, guess)
+    ]
     per = max(1, nbins * nmode // n)
     dims = (length, nvar, ctile, nblock, nbins, nmode, n_x, n_y, per, grid_points)
     y, z = pl.pallas_call(
@@ -262,9 +273,16 @@
             jax.ShapeDtypeStruct((nbins, 2 * nblock, points), jnp.bfloat16),
             jax.ShapeDtypeStruct((nbins * nmode, LANES), jnp.float32),
         ),
-        in_specs=[vmem] * 4,
+        in_specs=[hbm] * 5,
         out_specs=(vmem, vmem),
         scratch_shapes=[
+            pltpu.SMEM(starts.shape, jnp.int32),
+            pltpu.SMEM(bins.shape, jnp.int32),
+            pltpu.VMEM(x.shape, jnp.bfloat16),
+            pltpu.VMEM(quad_weight.shape, jnp.float32),
+            pltpu.VMEM(guess.shape, jnp.float32),
+            pltpu.VMEM((nblock * nq, length), jnp.bfloat16),
+            pltpu.VMEM((nq, NFFT), jnp.float32),
             pltpu.VMEM((length * ctile, cols_y), jnp.float32),
             pltpu.VMEM((length, points), jnp.bfloat16),
             pltpu.VMEM((1, LANES), jnp.float32),
@@ -273,12 +291,13 @@
             pltpu.VMEM((n, per, LANES), jnp.float32),
             pltpu.VMEM((n, per, LANES), jnp.float32),
             pltpu.VMEM((n, per, LANES), jnp.float32),
+            pltpu.SemaphoreType.DMA((5,)),
             pltpu.SemaphoreType.DMA((6,)),
         ],
         compiler_params=pltpu.CompilerParams(
             collective_id=0, has_side_effects=True, vmem_limit_bytes=limit
         ),
-    )(t, x, quad_weight, guess)
+    )(*operands)
 
     modes, energy = pl.pallas_call(
         functools.partial(modes_kernel, (ctile, nblock, nbins, nmode)),

time: 34.4 us -> 33.5 us (0.974)
  local copies, waits for them, and re-layouts: 1.44 us -> 0 us
  Pallas kernels: 32.1 us -> 32.7 us
    pallas_call x1, Pallas kernels: 27.1 us -> 30.3 us  [shards(): pl.pallas_call(functools.partial(main_kernel, dims), name='spod', out_sha...]
    pallas_call x1 -> x0, Pallas kernels: 2.54 us -> none  [shards(): pl.pallas_call(functools.partial(twiddle_kernel, (nblock, nbins)), name='...]
    unnamed x10 -> x0, local copies, waits for them, and re-layouts: 1.44 us -> none
where the time goes in v3:
time: 33.5 us; the launch traced here: 33.3 us
  Pallas kernels  32.7 us (98%)
  between operations  0.64 us (2%)
    pallas_call x1, Pallas kernels, shards(): pl.pallas_call(functools.partial(main_kernel, dims), name='spod', out_sha...  30.3 us
    pallas_call x1, Pallas kernels, shards(): pl.pallas_call(functools.partial(modes_kernel, (ctile, nblock, nbins, nmo...  2.39 us

profile of v3, /device:TPU:0, one launch (start us, length us, event | category | flops | bytes accessed | tf_op | source)
XLA Modules:
  0.0 33.3 jit_solution(1701652327274125876)
XLA Ops:
  0.6 30.3 %spod.1 = (bf16[16,128,768]{2,1,0:T(8,128)(2,1)S(1)}, f32[128,128]{1,0:T(8,128)S(1)}) custom-call(s32[64]{0:T(128)} %starts_hbm.1, s32[16]{0:T(128)} %bins_hbm.1, bf16[6144,128]{1,0:T(8,128)(2,1)} %bitcast.4, f32[3,2,128]{2,1,0:T(2,128)} %quad_hbm.1, f32[16,2,8,64]{3,2,1,0:T(8,128)} %bitcast.5), custom_call_target="tpu_custom_call" | custom-call | tf_op jit(solution)/shard_map/spod/pallas_call | solution.py:269
  30.9 2.4 %modes.1 = (f32[1536,128]{1,0:T(8,128)}, f32[8,16]{1,0:T(8,128)}) custom-call(bf16[16,128,768]{2,1,0:T(8,128)(2,1)S(1)} %get-tuple-element.6.y_ref, f32[128,128]{1,0:T(8,128)S(1)} %get-tuple-element.7.z_ref), custom_call_target="tpu_custom_call" | custom-call | tf_op jit(solution)/shard_map/modes/pallas_call | solution.py:302

commit v4 on v3

--- a/solution.py
+++ b/solution.py
@@ -57,7 +57,7 @@
 
 def main_kernel(dims, starts_hbm, bins_hbm, x_hbm, quad_hbm, guess_hbm, y_ref, z_ref,
                 starts, bins, x_ref, quad_ref, guess_ref, t_ref, tw, xs, xr, sq, qs,
-                sqbuf, zsend, zrecv, zall, load_sems, sems):
+                w_ref, acc, sqbuf, zsend, zrecv, zall, load_sems, sems):
     (length, nvar, ctile, nblock, nbins, nmode, n_x, n_y, per, grid_points) = dims
     n = n_x * n_y
     me = lax.axis_index("sx") * n_y + lax.axis_index("sy")
@@ -78,23 +78,33 @@
     for load in loads:
         load.start()
 
-    def coords(k):
-        t = lax.rem(me + k, n)
-        return t, (t // n_y, lax.rem(t, n_y))
+    ix, iy = lax.axis_index("sx"), lax.axis_index("sy")
+
+    def each_partner(act):
+        def pick(dx, dy):
+            tx, ty = lax.rem(ix + dx, n_x), lax.rem(iy + dy, n_y)
+            act(tx * n_y + ty, (tx, ty))
+
+        for dy in range(1, n_y):
+            pick(0, dy)
+
+        def go(dx, carry):
+            for dy in range(n_y):
+                pick(dx, dy)
+            return carry
+
+        lax.fori_loop(1, n_x, go, 0, unroll=5)
 
     barrier = pltpu.get_barrier_semaphore()
-
-    def greet(k, carry):
-        _, where = coords(k)
-        pl.semaphore_signal(barrier, inc=1, device_id=where, device_id_type=MESH)
-        return carry
-
-    lax.fori_loop(1, n, greet, 0)
+    each_partner(
+        lambda t, where: pl.semaphore_signal(
+            barrier, inc=1, device_id=where, device_id_type=MESH
+        )
+    )
 
     def spread(src, dst, phase, by_target):
-        def go(k, carry):
-            t, where = coords(k)
-            pltpu.make_async_remote_copy(
+        each_partner(
+            lambda t, where: pltpu.make_async_remote_copy(
                 src_ref=src.at[t] if by_target else src,
                 dst_ref=dst.at[me],
                 send_sem=sems.at[2 * phase],
@@ -102,9 +112,7 @@
                 device_id=where,
                 device_id_type=MESH,
             ).start()
-            return carry
-
-        lax.fori_loop(1, n, go, 0)
+        )
 
     def wait_all(dst, sem):
         rest = dst.at[pl.ds(0, n - 1)]
@@ -133,6 +141,18 @@
         total = total + jnp.where(lane == c // per_var, one, 0.0)
     sq[...] = total
 
+    for f in range(nbins):
+        g_re, g_im = guess_ref[f, 0], guess_ref[f, 1]
+        w_ref[f] = split2(
+            jnp.concatenate(
+                [
+                    jnp.concatenate([g_re, -g_im], axis=1),
+                    jnp.concatenate([g_im, g_re], axis=1),
+                ],
+                axis=0,
+            )
+        )
+
     pl.semaphore_wait(barrier, n - 1)
     spread(sq, sqbuf, 0, False)
 
@@ -144,18 +164,41 @@
                 starts[b], nq, length, tw
             )
 
-    chunk = nblock * nq // 4
-    for j in range(ctile // 2):
-        @pl.loop(0, 4)
-        def _(i):
-            at = pl.ds(pl.multiple_of(i * chunk, chunk), chunk)
-            out = jnp.dot(
-                t_ref[at, :],
-                xr[:, 2 * j * LANES:2 * (j + 1) * LANES],
-                preferred_element_type=jnp.float32,
+    chunks = 4
+    chunk = nblock * nq // chunks
+
+    def transform(i, j):
+        at = slice(i * chunk, (i + 1) * chunk)
+        out = jnp.dot(
+            t_ref[at, :],
+            xr[:, 2 * j * LANES:2 * (j + 1) * LANES],
+            preferred_element_type=jnp.float32,
+        )
+        qs[2 * j, at, :] = out[:, :LANES]
+        qs[2 * j + 1, at, :] = out[:, LANES:]
+
+    def fold(value):
+        return value[:2 * nmode] + value[2 * nmode:]
+
+    def project(f, j, cols):
+        for c in (2 * j, 2 * j + 1):
+            for p in range(2):
+                part = qs[c, pl.ds(p * nbins + f, nblock, stride=nq), :]
+                y_ref[f, p * nblock:(p + 1) * nblock, c * LANES:(c + 1) * LANES] = (
+                    part * cols[c]
+                ).astype(jnp.bfloat16)
+        y = y_ref[f, :, 2 * j * LANES:2 * (j + 1) * LANES]
+        u = fold(jnp.dot(w_ref[f], y, preferred_element_type=jnp.float32))
+        return fold(
+            lax.dot_general(
+                split2(u), y, (((1,), (1,)), ((), ())), preferred_element_type=jnp.float32
             )
-            qs[2 * j, at, :] = out[:, :LANES]
-            qs[2 * j + 1, at, :] = out[:, LANES:]
+        )
+
+    pairs = ctile // 2
+    share = nbins // chunks
+    for i in range(chunks):
+        transform(i, 0)
 
     wait_all(sqbuf, 1)
     sqbuf[me] = sq[...]
@@ -166,30 +209,20 @@
         one = jnp.sum(jnp.where(lane == c // per_var, scale, 0.0), axis=1, keepdims=True)
         cols.append(one * jnp.sqrt(quads[c]))
 
+    for j in range(1, pairs):
+        for i in range(chunks):
+            transform(i, j)
+            for f in range(i * share, (i + 1) * share):
+                a = project(f, j - 1, cols)
+                acc[f] = a if j == 1 else acc[f] + a
+
     low_half = lax.broadcasted_iota(jnp.int32, (nmode, LANES), 1) < nblock
     parts = nmode // per
     for f in range(nbins):
-        for c in range(ctile):
-            for p in range(2):
-                part = qs[c, pl.ds(p * nbins + f, nblock, stride=nq), :]
-                y_ref[f, p * nblock:(p + 1) * nblock, c * LANES:(c + 1) * LANES] = (
-                    part * cols[c]
-                ).astype(jnp.bfloat16)
-        y = y_ref[f]
-        g_re, g_im = guess_ref[f, 0], guess_ref[f, 1]
-        w = jnp.concatenate(
-            [
-                jnp.concatenate([g_re, -g_im], axis=1),
-                jnp.concatenate([g_im, g_re], axis=1),
-            ],
-            axis=0,
-        )
-        u = jnp.dot(split2(w), y, preferred_element_type=jnp.float32)
-        u = u[:2 * nmode] + u[2 * nmode:]
-        a = lax.dot_general(
-            split2(u), y, (((1,), (1,)), ((), ())), preferred_element_type=jnp.float32
-        )
-        a = (a[:2 * nmode] + a[2 * nmode:]) * (1.0 / (3.0 * grid_points))
+        a = project(f, pairs - 1, cols)
+        if pairs > 1:
+            a = a + acc[f]
+        a = a * (1.0 / (3.0 * grid_points))
         up = a[:nmode]
         z = pltpu.roll(a[nmode:], nblock, 1) + jnp.where(low_half, up, -up)
         for s in range(parts):
@@ -287,6 +320,8 @@
             pltpu.VMEM((length, points), jnp.bfloat16),
             pltpu.VMEM((1, LANES), jnp.float32),
             pltpu.VMEM((ctile, nblock * nq, LANES), jnp.float32),
+            pltpu.VMEM((nbins, 4 * nmode, 2 * nblock), jnp.bfloat16),
+            pltpu.VMEM((nbins, 2 * nmode, LANES), jnp.float32),
             pltpu.VMEM((n, 1, LANES), jnp.float32),
             pltpu.VMEM((n, per, LANES), jnp.float32),
             pltpu.VMEM((n, per, LANES), jnp.float32),

time: 33.5 us -> 32.4 us (0.967)
  Pallas kernels: 32.7 us -> 31.6 us
    pallas_call x1, Pallas kernels: 30.3 us -> 29.2 us  [shards(): pl.pallas_call(functools.partial(main_kernel, dims), name='spod', out_sha...]
where the time goes in v4:
time: 32.4 us; the launch traced here: 32.3 us
  Pallas kernels  31.6 us (98%)
  between operations  0.64 us (2%)
    pallas_call x1, Pallas kernels, shards(): pl.pallas_call(functools.partial(main_kernel, dims), name='spod', out_sha...  29.2 us
    pallas_call x1, Pallas kernels, shards(): pl.pallas_call(functools.partial(modes_kernel, (ctile, nblock, nbins, nmo...  2.39 us

profile of v4, /device:TPU:0, one launch (start us, length us, event | category | flops | bytes accessed | tf_op | source)
XLA Modules:
  0.0 32.3 jit_solution(5188539628773465266)
XLA Ops:
  0.6 29.2 %spod.1 = (bf16[16,128,768]{2,1,0:T(8,128)(2,1)S(1)}, f32[128,128]{1,0:T(8,128)S(1)}) custom-call(s32[64]{0:T(128)} %starts_hbm.1, s32[16]{0:T(128)} %bins_hbm.1, bf16[6144,128]{1,0:T(8,128)(2,1)} %bitcast.4, f32[3,2,128]{2,1,0:T(2,128)} %quad_hbm.1, f32[16,2,8,64]{3,2,1,0:T(8,128)} %bitcast.5), custom_call_target="tpu_custom_call" | custom-call | tf_op jit(solution)/shard_map/spod/pallas_call | solution.py:302
  29.9 2.4 %modes.1 = (f32[1536,128]{1,0:T(8,128)}, f32[8,16]{1,0:T(8,128)}) custom-call(bf16[16,128,768]{2,1,0:T(8,128)(2,1)S(1)} %get-tuple-element.6.y_ref, f32[128,128]{1,0:T(8,128)S(1)} %get-tuple-element.7.z_ref), custom_call_target="tpu_custom_call" | custom-call | tf_op jit(solution)/shard_map/modes/pallas_call | solution.py:337

commit v5 on v4

--- a/solution.py
+++ b/solution.py
@@ -167,15 +167,17 @@
     chunks = 4
     chunk = nblock * nq // chunks
 
-    def transform(i, j):
-        at = slice(i * chunk, (i + 1) * chunk)
-        out = jnp.dot(
-            t_ref[at, :],
-            xr[:, 2 * j * LANES:2 * (j + 1) * LANES],
-            preferred_element_type=jnp.float32,
-        )
-        qs[2 * j, at, :] = out[:, :LANES]
-        qs[2 * j + 1, at, :] = out[:, LANES:]
+    def transform(j):
+        @pl.loop(0, chunks)
+        def _(i):
+            at = pl.ds(pl.multiple_of(i * chunk, chunk), chunk)
+            out = jnp.dot(
+                t_ref[at, :],
+                xr[:, 2 * j * LANES:2 * (j + 1) * LANES],
+                preferred_element_type=jnp.float32,
+            )
+            qs[2 * j, at, :] = out[:, :LANES]
+            qs[2 * j + 1, at, :] = out[:, LANES:]
 
     def fold(value):
         return value[:2 * nmode] + value[2 * nmode:]
@@ -196,9 +198,8 @@
         )
 
     pairs = ctile // 2
-    share = nbins // chunks
-    for i in range(chunks):
-        transform(i, 0)
+    for j in range(pairs):
+        transform(j)
 
     wait_all(sqbuf, 1)
     sqbuf[me] = sq[...]
@@ -209,12 +210,10 @@
         one = jnp.sum(jnp.where(lane == c // per_var, scale, 0.0), axis=1, keepdims=True)
         cols.append(one * jnp.sqrt(quads[c]))
 
-    for j in range(1, pairs):
-        for i in range(chunks):
-            transform(i, j)
-            for f in range(i * share, (i + 1) * share):
-                a = project(f, j - 1, cols)
-                acc[f] = a if j == 1 else acc[f] + a
+    for j in range(pairs - 1):
+        for f in range(nbins):
+            a = project(f, j, cols)
+            acc[f] = a if j == 0 else acc[f] + a
 
     low_half = lax.broadcasted_iota(jnp.int32, (nmode, LANES), 1) < nblock
     parts = nmode // per

time: 32.4 us -> 33.1 us (1.022)
  Pallas kernels: 31.6 us -> 32.2 us
    pallas_call x1, Pallas kernels: 29.2 us -> 29.9 us  [shards(): pl.pallas_call(functools.partial(main_kernel, dims), name='spod', out_sha...]
where the time goes in v5:
time: 33.1 us; the launch traced here: 32.9 us
  Pallas kernels  32.2 us (97%)
  between operations  0.64 us (2%)
    pallas_call x1, Pallas kernels, shards(): pl.pallas_call(functools.partial(main_kernel, dims), name='spod', out_sha...  29.9 us
    pallas_call x1, Pallas kernels, shards(): pl.pallas_call(functools.partial(modes_kernel, (ctile, nblock, nbins, nmo...  2.39 us

profile of v5, /device:TPU:0, one launch (start us, length us, event | category | flops | bytes accessed | tf_op | source)
XLA Modules:
  0.0 32.9 jit_solution(13474411152290591012)
XLA Ops:
  0.6 29.9 %spod.1 = (bf16[16,128,768]{2,1,0:T(8,128)(2,1)S(1)}, f32[128,128]{1,0:T(8,128)S(1)}) custom-call(s32[64]{0:T(128)} %starts_hbm.1, s32[16]{0:T(128)} %bins_hbm.1, bf16[6144,128]{1,0:T(8,128)(2,1)} %bitcast.4, f32[3,2,128]{2,1,0:T(2,128)} %quad_hbm.1, f32[16,2,8,64]{3,2,1,0:T(8,128)} %bitcast.5), custom_call_target="tpu_custom_call" | custom-call | tf_op jit(solution)/shard_map/spod/pallas_call | solution.py:301
  30.5 2.4 %modes.1 = (f32[1536,128]{1,0:T(8,128)}, f32[8,16]{1,0:T(8,128)}) custom-call(bf16[16,128,768]{2,1,0:T(8,128)(2,1)S(1)} %get-tuple-element.6.y_ref, f32[128,128]{1,0:T(8,128)S(1)} %get-tuple-element.7.z_ref), custom_call_target="tpu_custom_call" | custom-call | tf_op jit(solution)/shard_map/modes/pallas_call | solution.py:336
